TPU v7x, 256 devices: a whole 4x4x8 slice. The times are simulated.
256 devices in a mesh: blk: 32 (over y, z_lo, core), grp: 8 (over z_hi, x).
Axes of the slice: x: 4, y: 4, z: 8 (z_hi: 2, z_lo: 4; z = z_hi * 4 + z_lo), core: 2. Of those that a mesh axis runs over, the one named last changes fastest.
Arguments:
- samples: float32 [128, 256, 256], P('blk', 'grp'), may hold values from -11 to 11
- pair_table: int32 [128, 16], P('blk'), may hold values from 0 to 127
- assignment: int32 [2, 128], P(None, 'blk'), may hold values from 0 to 255
- band_index: int32 [2], replicated, may hold values from 0 to 1023
Outputs:
- log_weight: float32 [2, 128, 256], P(None, 'blk', 'grp')
All inputs are finite; a program needn't handle non-finite values.
Results may differ from a plain program's by a relative error of at most 0.0003.
Values sent between devices are 32-bit elements; how exact they have to be, the bound alone decides.
A program may use at most 128 MiB of HBM per device.

v0:
```python
import functools

import jax
import jax.numpy as jnp
from jax import lax
from jax.sharding import Mesh
from jax.sharding import PartitionSpec as P

PAIRS = 16
GRP = ("grp_0", "grp_1")
BLK = ("blk_0", "blk_1", "blk_2")
BLK_GRP = ("blk_0", "blk_1", "blk_2", "grp_0", "grp_1")


def over_axes(shard, axes):
    return functools.reduce(lax.psum, axes, shard)


def laid_out(pieces, dim):
    pieces = jnp.moveaxis(pieces, 0, dim)
    lengths = pieces.shape
    return pieces.reshape(*lengths[:dim], lengths[dim] * lengths[dim + 1], *lengths[dim + 2 :])


def from_everyone(shard, axis):
    devices = lax.axis_size(axis)
    return lax.all_to_all(
        jnp.broadcast_to(shard[None], (devices, *shard.shape)), axis, 0, 0, tiled=True
    )


def gathered_copies(shard, axis, dim):
    return laid_out(from_everyone(shard, axis), dim)


def all_blocks(shard, axes, sequence):
    pieces = shard
    for k in sequence:
        pieces = lax.all_gather(pieces, axes[k])
    done = sequence[::-1]
    back = [done.index(k) for k in range(len(axes))]
    pieces = pieces.transpose(*back, *range(len(axes), pieces.ndim))
    return pieces.reshape(-1, *shard.shape)


def whole_of(shard, axes, sequence, dim):
    return laid_out(all_blocks(shard, axes, sequence), dim)


def collected_together(shard, axis):
    leaves = jax.tree.leaves(shard)
    sequence = sorted(range(len(leaves)), key=lambda k: -leaves[k].size)
    width = (1, *leaves[sequence[0]].shape)[-1]
    lines = [
        jnp.pad(leaves[k].reshape(-1), (0, -leaves[k].size % width)).reshape(-1, width)
        for k in sequence
    ]
    both, at, found = (from_everyone(jnp.concatenate(lines), axis), 0, {})
    for k, line in zip(sequence, lines):
        piece = both[:, at : at + len(line)].reshape(len(both), -1)
        found[k] = piece[:, : leaves[k].size].reshape(-1, *leaves[k].shape)
        at += len(line)
    numbers = iter(range(len(leaves)))
    return jax.tree.map(lambda _: found[next(numbers)], shard)


def combined_pairwise(pieces, combine):
    while len(jax.tree.leaves(pieces)[0]) > 1:
        pieces = jax.vmap(combine)(
            *(jax.tree.map(lambda part: part[side::2], pieces) for side in (0, 1))
        )
    return jax.tree.map(lambda part: part[0], pieces)


def combined_all(shard, axis, combine):
    pieces = collected_together(shard, axis)
    return combined_pairwise(pieces, combine)


def make_fold(queries, query_norm, band_list, counts):

    def fold(state, shard_rows, offset):
        count_in = shard_rows.shape[0]
        rows_dev = shard_rows.shape[1]

        def compute(inner):
            key_rows = shard_rows.reshape(count_in * rows_dev, shard_rows.shape[2])
            key_norm = jnp.sum(key_rows * key_rows, -1)
            product = jnp.einsum("qd,kd->qk", queries, key_rows, precision=lax.Precision.HIGHEST)
            distance = query_norm[:, None] + key_norm[None, :] - 2.0 * product
            blocks = []
            for band_sq in band_list:
                scores = (-distance / (2.0 * band_sq)).reshape(
                    distance.shape[0], count_in, rows_dev
                )
                peak = jnp.max(scores, -1)
                blocks.append(peak + jnp.log(jnp.sum(jnp.exp(scores - peak[..., None]), -1)))
            update = jnp.stack(blocks)
            return lax.dynamic_update_slice(inner, update, (0, 0, offset))

        needed = jnp.any(counts > 0)
        return lax.cond(needed, compute, lambda inner: inner, state)

    return fold


def per_device(samples, pair_table, assignment, band_index):
    local_subs, rows_dev, width = samples.shape
    rounds = assignment.shape[0]
    group_size = lax.axis_size(GRP)
    group_index = lax.axis_index(GRP)
    members = local_subs * lax.axis_size(BLK)
    band_sq = width * (1.0 + band_index.astype(jnp.float32) / 256.0) / 32.0
    local_pick = assignment - group_index * rows_dev
    onehot = (
        local_pick[:, :, None] == jnp.arange(rows_dev, dtype=jnp.int32)[None, None, :]
    ).astype(jnp.float32)
    picked = jnp.einsum("tsr,srd->td", onehot, samples, precision=lax.Precision.HIGHEST)
    centre = over_axes(picked, BLK_GRP) / members
    member_ids = jnp.arange(members, dtype=jnp.int32)
    count_int = jnp.sum(
        (pair_table[:, :, None] == member_ids[None, None, :]).astype(jnp.int32), axis=1
    )
    counts = count_int.astype(jnp.float32)
    gathered = gathered_copies(samples, GRP, 1)
    query_count = local_subs * rows_dev * group_size
    queries = gathered.reshape(query_count, width)
    query_norm = jnp.sum(queries * queries, -1)
    start_state = jnp.zeros((rounds, query_count, members), jnp.float32)
    fold = make_fold(queries, query_norm, [band_sq[turn] for turn in range(rounds)], count_int)
    partial_value = fold(start_state, whole_of(samples, BLK, (1, 0, 2), 0), jnp.int32(0))
    split_view = partial_value.reshape(rounds, local_subs, group_size, rows_dev, members)
    swapped = lax.all_to_all(split_view, GRP, split_axis=2, concat_axis=2, tiled=True)
    peak = jnp.max(swapped, 2)
    kernel = peak + jnp.log(jnp.sum(jnp.exp(swapped - peak[:, :, None]), 2))
    weighted = jnp.einsum("tsrm,sm->tsr", kernel, counts, precision=lax.Precision.HIGHEST) / PAIRS
    spread = samples[None] - centre[:, None, None, :]
    logits = weighted - jnp.sum(spread * spread, -1) / (2.0 * band_sq[:, None, None])
    row_peak = jnp.max(logits, -1)
    row_total = jnp.sum(jnp.exp(logits - row_peak[..., None]), -1)

    def combine_pair(first, second):
        joined = jnp.maximum(first[0], second[0])
        return (
            joined,
            first[1] * jnp.exp(first[0] - joined) + second[1] * jnp.exp(second[0] - joined),
        )

    peak_all, total_all = combined_all((row_peak, row_total), GRP, combine_pair)
    return logits - peak_all[..., None] - jnp.log(total_all)[..., None]


def solution(mesh):
    finer = Mesh(mesh.devices.reshape(4, 4, 2, 2, 4), ("blk_0", "blk_1", "blk_2", "grp_0", "grp_1"))
    return jax.shard_map(
        per_device,
        mesh=finer,
        in_specs=(P(BLK, GRP, None), P(BLK, None), P(None, BLK), P()),
        out_specs=P(None, BLK, GRP),
        check_vma=False,
    )
```

profile of v0, /device:TPU:1, one launch (start us, length us, event | category | flops | bytes accessed | tf_op | source)
XLA Modules:
  0.0 280.4 jit_solution(542961848151886727)
XLA Ops:
  6.5 17.4 %all-gather = f32[16,32,256]{2,1,0:T(8,128)} all-gather(f32[4,32,256]{2,1,0:T(8,128)} %param.6), channel_id=2, replica_groups=mesh['blk_0'=4,'blk_1'=4,'blk_2'=2,'grp_0'=2,'grp_1'=4] {'blk_1'}, dimensions={0}, use_global_device_ids=true | all-gather | bytes 655360 | tf_op jit(solution)/shard_map/all_gather | solution.py:39
  24.0 36.1 %all-gather.6.cloned.1.call-done = f32[16,4,32,256]{3,2,1,0:T(8,128)} async-done(((f32[4,4,32,256]{3,2,1,0:T(8,128)}), f32[16,4,32,256]{3,2,1,0:T(8,128)}) %all-gather.6.cloned.1.call-update) | async-done | bytes 2097168 | tf_op jit(solution)/shard_map/all_gather | solution.py:39
  60.2 2.0 broadcast_in_dim.6
  62.2 9.1 %all-to-all-start = ((f32[8,4,32,256]{3,2,1,0:T(8,128)}), f32[8,4,32,256]{3,2,1,0:T(8,128)S(1)}, u32[]{:S(2)}, u32[]{:S(2)}) async-start(f32[8,4,32,256]{3,2,1,0:T(8,128)} %broadcast_in_dim.6), calls=%async_computation | async-start | bytes 2097152 | tf_op jit(solution)/shard_map/all_to_all | solution.py:27
  71.4 0.8 convert_reduce_fusion
  74.1 17.9 %all-to-all-done = f32[8,4,32,256]{3,2,1,0:T(8,128)S(1)} async-done(((f32[8,4,32,256]{3,2,1,0:T(8,128)}), f32[8,4,32,256]{3,2,1,0:T(8,128)S(1)}, u32[]{:S(2)}, u32[]{:S(2)}) %all-to-all-start) | async-done | bytes 1048608 | tf_op jit(solution)/shard_map/all_to_all | solution.py:27
  92.1 107.8 %conditional.1 = (f32[2,1024,128]{1,2,0:T(8,128)S(1)}) conditional(s32[]{:T(128)} %convert_element_type.15, () %tuple.14, (f32[4,8,32,256]{3,2,0,1:T(8,128)S(1)}, f32[4,4,2,4,32,256]{5,4,3,1,0,2:T(8,128)}, f32[2]{0:T(128)S(1)}) %tuple.38), branch_computations={%region_2.0_spmd, %region_3.10_spmd} | conditional | flops 12937849856 | bytes 191971392 | solution.py:102
  92.1 4.8 %multiply_reduce_fusion = (f32[4,4,2,4,32]{4,3,2,1,0:T(4,128)S(1)}, f32[4,4,2,4,32,256]{5,4,3,2,1,0:T(8,128)}) fusion(f32[4,4,2,4,32,256]{5,4,3,1,0,2:T(8,128)} %get-tuple-element.51), kind=kLoop, calls=%fused_computation.11 | loop fusion | flops 2093056 | bytes 8404992 | tf_op jit(solution)/shard_map/cond/branch_1_fun/reduce_sum | solution.py:88
  99.0 23.1 %fusion.5 = (f32[1024,4096]{1,0:T(8,128)}, f32[1024,4096]{1,0:T(8,128)}) fusion(f32[]{:T(128)} %bitcast.2, f32[4096]{0:T(1024)S(1)} %add.62, f32[1024]{0:T(1024)S(1)} %reduce_sum.68, f32[]{:T(128)} %bitcast.5, f32[1024,256]{1,0:T(8,128)S(1)} %bitcast.56, f32[4096,256]{1,0:T(8,128)} %bitcast.51), kind=kOutput, calls=%fused_computation.10 | convolution fusion | flops 12910067712 | bytes 38817800 | tf_op jit(solution)/shard_map/cond/branch_1_fun/qd,kd->qk/dot_general | solution.py:89
  122.1 17.4 %copy.22 = f32[1024,4096]{0,1:T(8,128)} copy(f32[1024,4096]{1,0:T(8,128)} %get-tuple-element.59) | data formatting | bytes 33554432 | tf_op jit(solution)/shard_map/cond/branch_1_fun/div | solution.py:93
  139.5 9.3 %bitcast_reduce_fusion.1 = f32[1024,128]{0,1:T(8,128)S(1)} fusion(f32[1024,4096]{0,1:T(8,128)} %copy.22), kind=kLoop, calls=%fused_computation.5 | loop fusion | flops 4063232 | bytes 17301504 | tf_op jit(solution)/shard_map/cond/branch_1_fun/reduce_max | solution.py:96
  148.8 11.8 %fusion.3 = f32[1024,128]{0,1:T(8,128)S(1)} fusion(f32[1024,4096]{0,1:T(8,128)} %copy.22, f32[1024,128]{0,1:T(8,128)S(1)} %bitcast_reduce_fusion.1), kind=kLoop, calls=%fused_computation.7 | loop fusion | flops 8257536 | bytes 17825792 | tf_op jit(solution)/shard_map/cond/branch_1_fun/reduce_sum | solution.py:97
  160.6 17.5 %copy.23 = f32[1024,4096]{0,1:T(8,128)} copy(f32[1024,4096]{1,0:T(8,128)} %get-tuple-element.60) | data formatting | bytes 33554432 | tf_op jit(solution)/shard_map/cond/branch_1_fun/div | solution.py:93
  178.1 9.3 %bitcast_reduce_fusion = f32[1024,128]{0,1:T(8,128)S(1)} fusion(f32[1024,4096]{0,1:T(8,128)} %copy.23), kind=kLoop, calls=%fused_computation.1 | loop fusion | flops 4063232 | bytes 17301504 | tf_op jit(solution)/shard_map/cond/branch_1_fun/reduce_max | solution.py:96
  187.4 11.8 %fusion.1 = f32[1024,128]{0,1:T(8,128)S(1)} fusion(f32[1024,4096]{0,1:T(8,128)} %copy.23, f32[1024,128]{0,1:T(8,128)S(1)} %bitcast_reduce_fusion), kind=kLoop, calls=%fused_computation.3 | loop fusion | flops 8257536 | bytes 17825792 | tf_op jit(solution)/shard_map/cond/branch_1_fun/reduce_sum | solution.py:97
  200.2 1.1 copy.27
  201.3 6.6 %all-to-all-start.1 = ((f32[2,4,8,32,128]{4,3,1,0,2:T(8,128)}), f32[2,4,8,32,128]{4,3,1,0,2:T(8,128)S(1)}, u32[]{:S(2)}, u32[]{:S(2)}) async-start(f32[2,4,8,32,128]{4,3,1,0,2:T(8,128)} %copy.27), calls=%async_computation.1 | async-start | bytes 2097152 | tf_op jit(solution)/shard_map/all_to_all | solution.py:133
  208.2 6.5 %psum.35 = f32[2,256]{1,0:T(2,128)S(1)} all-reduce(f32[2,256]{1,0:T(2,128)S(1)} %convolution_bitcast_fusion), channel_id=1, replica_groups=mesh['blk_0'=4,'blk_1'=4,'blk_2'=2,'grp_0'=2,'grp_1'=4] {'blk_0'}, use_global_device_ids=true, to_apply=%region_12.13 | all-reduce | flops 512 | bytes 4096 | tf_op jit(solution)/shard_map/psum | solution.py:16
  214.8 22.5 %psum.36 = f32[2,256]{1,0:T(2,128)S(1)} all-reduce(f32[2,256]{1,0:T(2,128)S(1)} %psum.35), channel_id=1, replica_groups=mesh['blk_0'=4,'blk_1'=4,'blk_2'=2,'grp_0'=2,'grp_1'=4] {'blk_1'}, use_global_device_ids=true, to_apply=%region_13.14 | all-reduce | flops 512 | bytes 4096 | tf_op jit(solution)/shard_map/psum | solution.py:16
  237.2 2.5 psum.37
  239.8 7.7 %psum.38 = f32[2,256]{1,0:T(2,128)S(1)} all-reduce(f32[2,256]{1,0:T(2,128)S(1)} %psum.37), channel_id=1, replica_groups=mesh['blk_0'=4,'blk_1'=4,'blk_2'=2,'grp_0'=2,'grp_1'=4] {'grp_0'}, use_global_device_ids=true, to_apply=%region_15.0 | all-reduce | flops 512 | bytes 4096 | tf_op jit(solution)/shard_map/psum | solution.py:16
  247.4 8.8 %psum.39 = f32[2,256]{1,0:T(2,128)S(1)} all-reduce(f32[2,256]{1,0:T(2,128)S(1)} %psum.38), channel_id=1, replica_groups=mesh['blk_0'=4,'blk_1'=4,'blk_2'=2,'grp_0'=2,'grp_1'=4] {'grp_1'}, use_global_device_ids=true, to_apply=%region_16.0 | all-reduce | flops 512 | bytes 4096 | tf_op jit(solution)/shard_map/psum | solution.py:16
  257.6 15.3 %all_to_all.15 = f32[8,4,4]{2,1,0:T(4,128)S(1)} all-to-all(f32[8,4,4]{2,1,0:T(4,128)S(1)} %broadcast_in_dim.7), channel_id=1, replica_groups=mesh['blk_0'=4,'blk_1'=4,'blk_2'=2,'grp_0'=2,'grp_1'=4] {'grp_0','grp_1'}, dimensions={0} | all-to-all | bytes 1024 | tf_op jit(solution)/shard_map/all_to_all | solution.py:27
  272.9 0.7 subtract_subtract_fusion
  (37 shorter events, 4.8 us)
Async XLA Ops:
  6.5 53.7 %all-gather.6.cloned.1.call-start = ((), (), s32[]{:S(2)}) async-start(), calls=%async_computation.3 | async-start | bytes 2621440 | tf_op jit(solution)/shard_map/all_gather | solution.py:39
  24.0 68.1 %all-gather.8.cloned.1.call-start = ((), (), s32[]{:S(2)}) async-start(), calls=%async_computation.4 | async-start | bytes 6291456 | tf_op jit(solution)/shard_map/all_gather | solution.py:39
  62.2 29.8 %all-to-all-start = ((f32[8,4,32,256]{3,2,1,0:T(8,128)}), f32[8,4,32,256]{3,2,1,0:T(8,128)S(1)}, u32[]{:S(2)}, u32[]{:S(2)}) async-start(f32[8,4,32,256]{3,2,1,0:T(8,128)} %broadcast_in_dim.6), calls=%async_computation | async-start | bytes 2097152 | tf_op jit(solution)/shard_map/all_to_all | solution.py:27
  92.0 115.8 %copy-start.1 = (s32[2,4]{1,0:T(2,128)S(1)}, s32[2,4]{1,0:T(2,128)}, u32[]{:S(2)}) copy-start(s32[2,4]{1,0:T(2,128)} %param.8) | copy-start | bytes 100
  92.0 115.9 %copy-start = (f32[4,32,256]{2,1,0:T(8,128)S(1)}, f32[4,32,256]{2,1,0:T(8,128)}, u32[]{:S(2)}) copy-start(f32[4,32,256]{2,1,0:T(8,128)} %param.6) | copy-start | bytes 393220
  201.3 55.1 %all-to-all-start.1 = ((f32[2,4,8,32,128]{4,3,1,0,2:T(8,128)}), f32[2,4,8,32,128]{4,3,1,0,2:T(8,128)S(1)}, u32[]{:S(2)}, u32[]{:S(2)}) async-start(f32[2,4,8,32,128]{4,3,1,0,2:T(8,128)} %copy.27), calls=%async_computation.1 | async-start | bytes 2097152 | tf_op jit(solution)/shard_map/all_to_all | solution.py:133
Sparse Core Ops, SparseCore 0:
  24.1 36.0 all-gather.5
  62.0 19.7 all-gather.7
where the time goes:
time: 284 us; the launch traced here: 280 us
  blocking collectives  80.7 us (28%)
  waiting for transfers between devices  54.1 us (19%)
  other arithmetic  51 us (18%)
  local copies, waits for them, and re-layouts  39.2 us (14%)
  matrix products  23.9 us (8%)
  starting transfers between devices  15.8 us (6%)
  between operations  14.2 us (5%)
    psum x5, blocking collectives, over_axes(): return functools.reduce(lax.psum, axes, shard)  48 us
    all_gather x2, waiting for transfers between devices, all_blocks(): pieces = lax.all_gather(pieces, axes[k])  36.1 us
    div x2, local copies, waits for them, and re-layouts, compute(): -distance / (2.0 * band_sq)  34.9 us
    reduce_sum x2, other arithmetic, compute(): jnp.sum(jnp.exp(scores - peak[..., None]), -1)  23.6 us
    dot_general x1, matrix products, compute(): jnp.einsum('qd,kd->qk', queries, key_rows, precision=lax.Precision.HIGHEST)  23.1 us
    reduce_max x2, other arithmetic, compute(): peak = jnp.max(scores, -1)  18.6 us
    all_to_all x1, waiting for transfers between devices, from_everyone(): lax.all_to_all(jnp.broadcast_to(shard[None], (devices, *shard.shape)), ax...  17.9 us
    all_gather x1, blocking collectives, all_blocks(): pieces = lax.all_gather(pieces, axes[k])  17.4 us
  transfers between devices with their start and end apart: 4, of which 2 were waited for; matrix products, arithmetic and copies ran while one was open for 2% of the time, Pallas kernels for 0%

commit v1 on v0

v1 whole, which is shorter than its diff:
```python
import functools
import math

import jax
import jax.numpy as jnp
from jax import lax
from jax.experimental import pallas as pl
from jax.experimental.pallas import tpu as pltpu
from jax.sharding import Mesh
from jax.sharding import PartitionSpec as P

MESH = pl.DeviceIdType.MESH
NAMES = ("y", "zl", "core", "zh", "x")
Y, ZL, CORES, ZH, X = 4, 4, 2, 2, 4
GROUP = ZH * X
SUBS, ROWS, D, ROUNDS, PAIRS, MEMBERS = 4, 32, 256, 2, 16, 128
DRAWS = GROUP * ROWS
TILES = SUBS * ROWS // 8 + 1
HALF = TILES // 2
LOG2E = math.log2(math.e)
LN2 = math.log(2.0)
NT = (((1,), (1,)), ((), ()))


def split(value):
    high = value.astype(jnp.bfloat16)
    low = (value - high.astype(jnp.float32)).astype(jnp.bfloat16)
    return high, low


def nt_dot(a, b):
    return lax.dot_general(a, b, NT, preferred_element_type=jnp.float32)


def row_sums(value):
    ones = jnp.ones((8, value.shape[1]), jnp.bfloat16)
    high, low = split(value)
    lowest = (value - high.astype(jnp.float32) - low.astype(jnp.float32)).astype(jnp.bfloat16)
    return (nt_dot(ones, high) + nt_dot(ones, low) + nt_dot(ones, lowest))[0:1]


def kernel(
    table, picks, bands, own, out,
    keys, queries, parts_hi, parts_lo, query_half, sums_out, sums_in, centre_out, centre_in, final_out, final_in,
    z_send, z_recv, y_send, y_recv, half_send, half_recv, sib_send, sib_recv,
    zh_send, zh_recv, x_send, x_recv, xhalf_send, xhalf_recv,
    c_send, c_recv, l_send, l_recv, f_send, f_recv,
):
    y, zl, core, zh, x = (lax.axis_index(name) for name in NAMES)
    me = zh * X + x

    def block(row, seg):
        return (row * ZL + seg) * CORES + core

    def device(**where):
        return where

    def copy(src, dst, send, recv, **where):
        made = pltpu.make_async_remote_copy(
            src_ref=src, dst_ref=dst, send_sem=send, recv_sem=recv, device_id=where, device_id_type=MESH
        )
        return made

    y_up, y_down = lax.rem(y + 1, Y), lax.rem(y + Y - 1, Y)
    x_up, x_down = lax.rem(x + 1, X), lax.rem(x + X - 1, X)
    segs = [lax.rem(zl + k, ZL) for k in range(ZL)]
    others = [(dz, dx) for dx in range(X) for dz in range(ZH) if (dz, dx) != (0, 0)]

    def peer(dz, dx):
        return lax.rem(zh + dz, ZH), lax.rem(x + dx, X)

    barrier = pltpu.get_barrier_semaphore()
    greeted = [{"zl": segs[k]} for k in range(1, ZL)]
    greeted += [{"y": y_up}, {"y": y_down}, {"core": 1 - core}]
    for dz, dx in others:
        to_zh, to_x = peer(dz, dx)
        greeted.append({"zh": to_zh, "x": to_x})
    for where in greeted:
        pl.semaphore_signal(barrier, inc=1, device_id=where, device_id_type=MESH)

    mine = block(y, zl)
    held = own[...]
    keys[mine, 0 : TILES - 1] = held.reshape(TILES - 1, 8, D)
    queries[me] = held
    number = lax.broadcasted_iota(jnp.int32, (ROWS, D), 0)
    chosen = []
    for t in range(ROUNDS):
        total = jnp.zeros((ROWS, D), jnp.float32)
        for m in range(SUBS):
            total += jnp.where(number == picks[t, m] - me * ROWS, held[m], 0.0)
        chosen.append(jnp.sum(total, 0, keepdims=True))
    line = lax.broadcasted_iota(jnp.int32, (8, D), 0)
    keys[mine, TILES - 1] = jnp.where(line == 0, chosen[0], jnp.where(line == 1, chosen[1], 0.0))

    pl.semaphore_wait(barrier, len(greeted))

    sends = []

    def go(made):
        made.start()
        sends.append(made)
        return made

    z_copies, y_copies, half_copies, sib_copies = [], {}, {}, []

    def to_sibling(b):
        n = len(sib_copies)
        sib_copies.append(
            go(copy(keys.at[b], keys.at[b], sib_send.at[n], sib_recv.at[n], core=1 - core))
        )

    def along_y(k):
        b = block(y, segs[k])
        for side, to in enumerate((y_up, y_down)):
            y_copies[k, side] = go(copy(keys.at[b], keys.at[b], y_send.at[k, side], y_recv.at[k, side], y=to))

    def along_y_again(k):
        for side, (source, to) in enumerate(((y_down, y_up), (y_up, y_down))):
            b = block(source, segs[k])
            y_copies[k, side].wait_recv()
            part = pl.ds(0, HALF) if side == 0 else pl.ds(HALF, TILES - HALF)
            half_copies[k, side] = go(
                copy(
                    keys.at[b, part], keys.at[b, part], half_send.at[k, side], half_recv.at[k, side], y=to
                )
            )
            to_sibling(b)

    along_y(0)
    for k in range(1, ZL):
        z_copies.append(
            go(copy(keys.at[mine], keys.at[mine], z_send.at[k - 1], z_recv.at[k - 1], zl=segs[k]))
        )
    zh_copy = go(copy(queries.at[me], queries.at[me], zh_send, zh_recv, zh=1 - zh))
    x_copies, xhalf_copies = {}, {}

    def along_x(k):
        slot = lax.rem(zh + k, ZH) * X + x
        for side, to in enumerate((x_up, x_down)):
            x_copies[k, side] = go(
                copy(queries.at[slot], queries.at[slot], x_send.at[k, side], x_recv.at[k, side], x=to)
            )

    def along_x_again(k):
        for side, (source, to) in enumerate(((x_down, x_up), (x_up, x_down))):
            slot = lax.rem(zh + k, ZH) * X + source
            x_copies[k, side].wait_recv()
            part = pl.ds(0, SUBS // 2) if side == 0 else pl.ds(SUBS // 2, SUBS // 2)
            xhalf_copies[k, side] = go(
                copy(
                    queries.at[slot, part], queries.at[slot, part],
                    xhalf_send.at[k, side], xhalf_recv.at[k, side], x=to,
                )
            )

    along_x(0)
    to_sibling(mine)

    def z_arrived(k):
        z_copies[k - 1].wait_recv()

    back = [lax.rem(zl + ZL - k, ZL) for k in range(ZL)]
    segs = back
    along_y_again(0)
    along_x_again(0)
    z_arrived(1)
    along_y(1)
    to_sibling(block(y, segs[1]))
    zh_copy.wait_recv()
    along_x(1)
    z_arrived(2)
    along_y(2)
    to_sibling(block(y, segs[2]))
    along_y_again(1)
    z_arrived(3)
    along_y(3)
    to_sibling(block(y, segs[3]))
    along_x_again(1)
    along_y_again(2)

    for made in xhalf_copies.values():
        made.wait_recv()
    for m in range(SUBS):
        whole = queries[:, m].reshape(DRAWS, D)
        high, low = split(whole)
        parts_hi[m] = high
        parts_lo[m] = low
        query_half[m] = jnp.broadcast_to(0.5 * row_sums(whole * whole), (8, DRAWS))

    along_y_again(3)
    far = lax.rem(y + 2, Y)
    for k in range(ZL):
        half_copies[k, 0].wait_recv()
        half_copies[k, 1].wait_recv()
        to_sibling(block(far, segs[k]))
    for made in sib_copies:
        made.wait_recv()

    total = keys[0, TILES - 1]
    for b in range(1, Y * ZL * CORES):
        total += keys[b, TILES - 1]
    centre_out[...] = total
    centre_in[me] = total
    c_copies = []
    for n, (dz, dx) in enumerate(others):
        to_zh, to_x = peer(dz, dx)
        c_copies.append(go(copy(centre_out, centre_in.at[me], c_send.at[n], c_recv.at[n], zh=to_zh, x=to_x)))

    scale = []
    for t in range(ROUNDS):
        index = jnp.full((1, DRAWS), bands[t], jnp.int32).astype(jnp.float32)
        scale.append((D / 32.0) * (1.0 + index / 256.0))

    l_copies = []
    slots = 8
    for k in range(X):
        m = lax.rem(x + 1 + k, X)
        high, low = parts_hi[m], parts_lo[m]
        shift = query_half[m, 0:1]
        for first in range(0, PAIRS, slots):
            rows = []
            for s in range(first, first + slots):
                p = table[m, s]
                b = lax.div(p, SUBS)
                q = lax.rem(p, SUBS) * (ROWS // 8)
                rows.append(keys[b, pl.ds(q, ROWS // 8)].reshape(ROWS, D))
            rows = jnp.concatenate(rows, 0)
            norm_half = 0.5 * jnp.sum(rows * rows, -1, keepdims=True)
            key_high, key_low = split(rows)
            product = nt_dot(key_high, high) + nt_dot(key_low, high) + nt_dot(key_high, low)
            value = (product - norm_half).reshape(slots, ROWS, DRAWS)
            peak = jnp.max(value, 1, keepdims=True)
            value = value - peak
            peak = peak.reshape(slots, DRAWS) - shift
            for t in range(ROUNDS):
                rate = LOG2E / scale[t]
                mass = jnp.sum(jnp.exp2(value * rate[None]), 1)
                sums_out[m, t, pl.ds(first, slots)] = peak * rate + jnp.log2(mass)
        for dz in range(ZH):
            if (dz, k) == (0, X - 1):
                sums_in[me] = sums_out[m, zh]
                continue
            n = len(l_copies)
            to_zh = lax.rem(zh + dz, ZH)
            l_copies.append(
                go(
                    copy(
                        sums_out.at[m, to_zh], sums_in.at[me], l_send.at[n], l_recv.at[n], zh=to_zh, x=m
                    )
                )
            )

    for made in c_copies:
        made.wait_recv()
    centre = jnp.sum(centre_in[:, pl.ds(zh, 1)].reshape(GROUP, D), 0, keepdims=True) / MEMBERS
    away = queries[:, x].reshape(DRAWS, D) - centre
    spread = row_sums(away * away)
    band = jnp.where(zh == 0, scale[0], scale[1])
    for made in l_copies:
        made.wait_recv()
    pieces = sums_in[...]
    peak = jnp.max(pieces, 0)
    whole = peak + jnp.log2(jnp.sum(jnp.exp2(pieces - peak[None]), 0))
    logits = (LN2 / PAIRS) * jnp.sum(whole, 0, keepdims=True) - spread / (2.0 * band)
    logits = logits - jnp.max(logits, -1, keepdims=True)
    result = logits - jnp.log(jnp.sum(jnp.exp(logits), -1, keepdims=True))
    for g in range(GROUP):
        final_out[g, 0:1, 0:ROWS] = result[:, g * ROWS : (g + 1) * ROWS]
    f_copies = []
    for n, (dz, dx) in enumerate(others):
        to_zh, to_x = peer(dz, dx)
        f_copies.append(
            go(
                copy(
                    final_out.at[to_zh * X + to_x], final_in.at[me], f_send.at[n], f_recv.at[n],
                    zh=to_zh, x=to_x,
                )
            )
        )
    final_in[me] = final_out[me]
    for made in f_copies:
        made.wait_recv()
    out[...] = final_in[:, 0, 0:ROWS].reshape(ROUNDS, SUBS, ROWS)
    for made in sends:
        made.wait_send()


def per_device(samples, pair_table, assignment, band_index):
    dma = pltpu.SemaphoreType.DMA
    smem = pl.BlockSpec(memory_space=pltpu.SMEM)
    vmem = pl.BlockSpec(memory_space=pltpu.VMEM)
    f32 = jnp.float32
    peers = GROUP - 1
    return pl.pallas_call(
        kernel,
        name="weights",
        out_shape=jax.ShapeDtypeStruct((ROUNDS, SUBS, ROWS), f32),
        in_specs=[smem, smem, smem, vmem],
        out_specs=vmem,
        scratch_shapes=[
            pltpu.VMEM((Y * ZL * CORES, TILES, 8, D), f32),
            pltpu.VMEM((GROUP, SUBS, ROWS, D), f32),
            pltpu.VMEM((SUBS, DRAWS, D), jnp.bfloat16),
            pltpu.VMEM((SUBS, DRAWS, D), jnp.bfloat16),
            pltpu.VMEM((SUBS, 8, DRAWS), f32),
            pltpu.VMEM((SUBS, ROUNDS, PAIRS, DRAWS), f32),
            pltpu.VMEM((GROUP, PAIRS, DRAWS), f32),
            pltpu.VMEM((8, D), f32),
            pltpu.VMEM((GROUP, 8, D), f32),
            pltpu.VMEM((GROUP, 8, 128), f32),
            pltpu.VMEM((GROUP, 8, 128), f32),
            dma((ZL - 1,)), dma((ZL - 1,)),
            dma((ZL, 2)), dma((ZL, 2)),
            dma((ZL, 2)), dma((ZL, 2)),
            dma((Y * ZL,)), dma((Y * ZL,)),
            dma, dma,
            dma((ZH, 2)), dma((ZH, 2)),
            dma((ZH, 2)), dma((ZH, 2)),
            dma((peers,)), dma((peers,)),
            dma((peers,)), dma((peers,)),
            dma((peers,)), dma((peers,)),
        ],
        compiler_params=pltpu.CompilerParams(
            collective_id=0, has_side_effects=True, vmem_limit_bytes=48 * 1024 * 1024
        ),
    )(pair_table, assignment, band_index, samples)


def solution(mesh):
    finer = Mesh(mesh.devices.reshape(Y, ZL, CORES, ZH, X), NAMES)
    blk, grp = NAMES[:3], NAMES[3:]
    return jax.shard_map(
        per_device,
        mesh=finer,
        in_specs=(P(blk, grp, None), P(blk, None), P(None, blk), P()),
        out_specs=P(None, blk, grp),
        check_vma=False,
    )
```

time: 284 us -> 61.5 us (0.22); the launches traced: 280 us -> 61.4 us
  blocking collectives: 80.7 us -> 0 us
  Pallas kernels: 0 us -> 57.8 us
  waiting for transfers between devices: 54.1 us -> 0 us
  other arithmetic: 51 us -> 0 us
  local copies, waits for them, and re-layouts: 39.2 us -> 3.51 us
  matrix products: 23.9 us -> 0 us
  starting transfers between devices: 15.8 us -> 0 us
  between operations: 14.2 us -> 0.01 us
    pallas_call x0 -> x1, Pallas kernels: none -> 57.8 us  [per_device(): pl.pallas_call(kernel, name='weights', out_shape=jax.ShapeDtypeStruct((RO...]
    psum x5 -> x0, blocking collectives: 48 us -> none  [over_axes(): return functools.reduce(lax.psum, axes, shard)]
    all_gather x2 -> x0, waiting for transfers between devices: 36.1 us -> none  [all_blocks(): pieces = lax.all_gather(pieces, axes[k])]
    div x2 -> x0, local copies, waits for them, and re-layouts: 34.9 us -> none  [compute(): -distance / (2.0 * band_sq)]
    reduce_sum x8 -> x0, other arithmetic: 29.8 us -> none  [the longest x2 23.6 us: compute(): jnp.sum(jnp.exp(scores - peak[..., None]), -1)]
    dot_general x3 -> x0, matrix products: 23.9 us -> none  [the longest x1 23.1 us: compute(): jnp.einsum('qd,kd->qk', queries, key_rows, precision=lax.Precision.HIGHEST)]
    reduce_max x4 -> x0, other arithmetic: 18.8 us -> none  [the longest x2 18.6 us: compute(): peak = jnp.max(scores, -1)]
    all_to_all x2 -> x0, waiting for transfers between devices: 17.9 us -> none  [the longest x1 17.9 us: from_everyone(): lax.all_to_all(jnp.broadcast_to(shard[None], (devices, *shard.shape)), ax...]
  transfers between devices with their start and end apart: 4 -> 0, of which waited for: 2 -> 0; matrix products, arithmetic and copies ran while one was open for 2% -> 0% of each run, Pallas kernels for 0% -> 0%
where the time goes in v1:
time: 61.5 us; the launch traced here: 61.4 us
  Pallas kernels  57.8 us (94%)
  local copies, waits for them, and re-layouts  3.51 us (6%)
    pallas_call x1, Pallas kernels, per_device(): pl.pallas_call(kernel, name='weights', out_shape=jax.ShapeDtypeStruct((RO...  57.8 us
    unnamed x9, local copies, waits for them, and re-layouts  3.51 us

profile of v1, /device:TPU:1, one launch (start us, length us, event | category | flops | bytes accessed | tf_op | source)
XLA Modules:
  0.0 61.4 jit_solution(11778605519609452938)
XLA Ops:
  0.0 0.0 copy-start
  0.0 0.9 %copy-done = f32[4,32,256]{2,1,0:T(8,128)S(1)} copy-done((f32[4,32,256]{2,1,0:T(8,128)S(1)}, f32[4,32,256]{2,1,0:T(8,128)}, u32[]{:S(2)}) %copy-start) | copy-done | bytes 131096
  0.9 0.0 copy-start.1
  0.9 0.7 %copy-done.1 = s32[4,16]{1,0:T(4,128)S(1)} copy-done((s32[4,16]{1,0:T(4,128)S(1)}, s32[4,16]{1,0:T(4,128)}, u32[]{:S(2)}) %copy-start.1) | copy-done | bytes 280
  1.6 0.0 copy-start.2
  1.6 0.7 %copy-done.2 = s32[2,4]{1,0:T(2,128)S(1)} copy-done((s32[2,4]{1,0:T(2,128)S(1)}, s32[2,4]{1,0:T(2,128)}, u32[]{:S(2)}) %copy-start.2) | copy-done | bytes 56
  2.3 0.0 copy-start.3
  2.3 0.7 %copy-done.3 = s32[2]{0:T(128)S(1)} copy-done((s32[2]{0:T(128)S(1)}, s32[2]{0:T(128)}, u32[]{:S(2)}) %copy-start.3) | copy-done | bytes 32
  2.9 57.8 %weights.1 = f32[2,4,32]{2,1,0:T(4,128)S(1)} custom-call(s32[4,16]{1,0:T(4,128)S(1)} %copy-done.1, s32[2,4]{1,0:T(2,128)S(1)} %copy-done.2, s32[2]{0:T(128)S(1)} %copy-done.3, f32[4,32,256]{2,1,0:T(8,128)S(1)} %copy-done), custom_call_target="tpu_custom_call" | custom-call | tf_op jit(solution)/shard_map/weights/pallas_call | solution.py:294
  60.8 0.6 copy.6
Async XLA Ops:
  0.0 0.9 %copy-start = (f32[4,32,256]{2,1,0:T(8,128)S(1)}, f32[4,32,256]{2,1,0:T(8,128)}, u32[]{:S(2)}) copy-start(f32[4,32,256]{2,1,0:T(8,128)} %own.1) | copy-start | bytes 393220
  0.9 0.7 %copy-start.1 = (s32[4,16]{1,0:T(4,128)S(1)}, s32[4,16]{1,0:T(4,128)}, u32[]{:S(2)}) copy-start(s32[4,16]{1,0:T(4,128)} %table.1) | copy-start | bytes 772
  1.6 0.7 %copy-start.2 = (s32[2,4]{1,0:T(2,128)S(1)}, s32[2,4]{1,0:T(2,128)}, u32[]{:S(2)}) copy-start(s32[2,4]{1,0:T(2,128)} %picks.1) | copy-start | bytes 100
  2.3 0.7 %copy-start.3 = (s32[2]{0:T(128)S(1)}, s32[2]{0:T(128)}, u32[]{:S(2)}) copy-start(s32[2]{0:T(128)} %bands.1) | copy-start | bytes 28

commit v2 on v1

v2 whole, which is shorter than its diff:
```python
import math

import jax
import jax.numpy as jnp
from jax import lax
from jax.experimental import pallas as pl
from jax.experimental.pallas import tpu as pltpu
from jax.sharding import Mesh
from jax.sharding import PartitionSpec as P

MESH = pl.DeviceIdType.MESH
NAMES = ("y", "zl", "core", "zh", "x")
Y, ZL, CORES, ZH, X = 4, 4, 2, 2, 4
GROUP = ZH * X
SUBS, ROWS, D, ROUNDS, PAIRS, MEMBERS = 4, 32, 256, 2, 16, 128
DRAWS = GROUP * ROWS
HALF = SUBS // 2
SLOTS = 8
LOG2E = math.log2(math.e)
LN2 = math.log(2.0)
NT = (((1,), (1,)), ((), ()))


def split(value):
    high = value.astype(jnp.bfloat16)
    low = (value - high.astype(jnp.float32)).astype(jnp.bfloat16)
    return high, low


def nt_dot(a, b):
    return lax.dot_general(a, b, NT, preferred_element_type=jnp.float32)


def row_sums(value):
    ones = jnp.ones((8, value.shape[1]), jnp.bfloat16)
    high, low = split(value)
    lowest = (value - high.astype(jnp.float32) - low.astype(jnp.float32)).astype(jnp.bfloat16)
    return (nt_dot(ones, high) + nt_dot(ones, low) + nt_dot(ones, lowest))[0:1]


def log_sum(pieces):
    peak = jnp.max(pieces, 0)
    return peak + jnp.log2(jnp.sum(jnp.exp2(pieces - peak[None]), 0))


def kernel(
    table, picks, bands, own, out,
    keys, queries, parts_hi, parts_lo, query_half, sums_out, sums_in, pair_out, pair_in,
    pick_out, pick_in, final_out, final_in,
    z_send, z_recv, y_send, y_recv, half_send, half_recv, sib_send, sib_recv,
    zh_send, zh_recv, x_send, x_recv, xhalf_send, xhalf_recv,
    p_send, p_recv, l_send, l_recv, pair_send, pair_recv, f_send, f_recv,
):
    y, zl, core, zh, x = (lax.axis_index(name) for name in NAMES)
    me = zh * X + x

    def block(row, seg):
        return (row * ZL + seg) * CORES + core

    def copy(src, dst, send, recv, **where):
        return pltpu.make_async_remote_copy(
            src_ref=src, dst_ref=dst, send_sem=send, recv_sem=recv, device_id=where, device_id_type=MESH
        )

    y_up, y_down, y_far = (lax.rem(y + k, Y) for k in (1, 3, 2))
    x_up, x_down, x_far = (lax.rem(x + k, X) for k in (1, 3, 2))

    barrier = pltpu.get_barrier_semaphore()
    greeted = [{"core": 1 - core}, {"zh": 1 - zh}]
    greeted += [{"zl": lax.rem(zl + k, ZL)} for k in range(1, ZL)]
    greeted += [{"y": k} for k in (y_up, y_down, y_far)]
    greeted += [{"x": k} for k in (x_up, x_down, x_far)]
    for where in greeted:
        pl.semaphore_signal(barrier, inc=1, device_id=where, device_id_type=MESH)

    mine = block(y, zl)
    held = own[...]
    keys[mine] = held
    queries[me] = held
    number = lax.broadcasted_iota(jnp.int32, (ROWS, D), 0)
    pick_out[0] = jnp.zeros((8, 128), jnp.float32)
    for t in range(ROUNDS):
        total = jnp.zeros((ROWS, D), jnp.float32)
        for m in range(SUBS):
            total += jnp.where(number == picks[t, m] - me * ROWS, held[m], 0.0)
        total = jnp.sum(total, 0, keepdims=True)
        for side in range(2):
            pick_out[0, 2 * t + side : 2 * t + side + 1] = total[:, 128 * side : 128 * side + 128]

    pl.semaphore_wait(barrier, len(greeted))

    sends = []

    def go(made):
        made.start()
        sends.append(made)
        return made

    low = zl < 2
    segs = [zl, zl + 1 - 2 * lax.rem(zl, 2), jnp.where(low, 2, 1), jnp.where(low, 3, 0)]
    y_copies, half_copies, sib_copies = {}, {}, []

    def to_sibling(*where):
        n = len(sib_copies)
        part = keys.at[where]
        sib_copies.append(go(copy(part, part, sib_send.at[n], sib_recv.at[n], core=1 - core)))

    def z_copy(seg, up):
        b = block(y, seg)
        return copy(
            keys.at[b], keys.at[b], z_send.at[seg, int(up)], z_recv.at[seg], zl=zl + 1 if up else zl - 1
        )

    def along_y(k):
        b = block(y, segs[k])
        for side, to in enumerate((y_up, y_down)):
            y_copies[k, side] = go(copy(keys.at[b], keys.at[b], y_send.at[k, side], y_recv.at[k, side], y=to))
        to_sibling(b)

    def along_y_again(k):
        for side, (source, to) in enumerate(((y_down, y_up), (y_up, y_down))):
            b = block(source, segs[k])
            y_copies[k, side].wait_recv()
            part = keys.at[b, pl.ds(side * HALF, HALF)]
            half_copies[k, side] = go(copy(part, part, half_send.at[k, side], half_recv.at[k, side], y=to))
            to_sibling(b)

    def far_arrived(k):
        for side in range(2):
            half_copies[k, side].wait_recv()
            to_sibling(block(y_far, segs[k]), pl.ds(side * HALF, HALF))

    def z_arrived(k):
        seg = segs[k]
        z_copy(seg, True).wait_recv()

        @pl.when((seg < zl) & (zl < ZL - 1))
        def _():
            z_copy(seg, True).start()

        @pl.when((seg > zl) & (zl > 0))
        def _():
            z_copy(seg, False).start()

    def z_sent(k):
        seg = segs[k]

        @pl.when((seg <= zl) & (zl < ZL - 1))
        def _():
            z_copy(seg, True).wait_send()

        @pl.when((seg >= zl) & (zl > 0))
        def _():
            z_copy(seg, False).wait_send()

    x_copies, xhalf_copies = {}, {}

    def along_x(k):
        slot = lax.rem(zh + k, ZH) * X + x
        for side, to in enumerate((x_up, x_down)):
            x_copies[k, side] = go(
                copy(queries.at[slot], queries.at[slot], x_send.at[k, side], x_recv.at[k, side], x=to)
            )

    def along_x_again(k):
        for side, (source, to) in enumerate(((x_down, x_up), (x_up, x_down))):
            slot = lax.rem(zh + k, ZH) * X + source
            x_copies[k, side].wait_recv()
            part = queries.at[slot, pl.ds(side * HALF, HALF)]
            xhalf_copies[k, side] = go(copy(part, part, xhalf_send.at[k, side], xhalf_recv.at[k, side], x=to))

    axes = [
        [{"core": 1 - core}],
        [{"zl": lax.rem(zl + k, ZL)} for k in range(1, ZL)],
        [{"y": lax.rem(y + k, Y)} for k in range(1, Y)],
        [{"x": lax.rem(x + k, X)} for k in range(1, X)],
        [{"zh": 1 - zh}],
    ]
    pick_copies = {}

    def picks_along(a):
        for n, where in enumerate(axes[a]):
            pick_copies[a, n] = go(
                copy(pick_out.at[a], pick_in.at[a, n], p_send.at[a, n], p_recv.at[a, n], **where)
            )

    def picks_arrived(a):
        total = pick_out[a]
        for n in range(len(axes[a])):
            pick_copies[a, n].wait_recv()
            total += pick_in[a, n]
        pick_out[a + 1] = total

    @pl.when(zl < ZL - 1)
    def _():
        z_copy(zl, True).start()

    @pl.when(zl > 0)
    def _():
        z_copy(zl, False).start()

    along_y(0)
    along_x(0)
    picks_along(0)
    picks_arrived(0)
    picks_along(1)
    z_arrived(1)
    along_y(1)
    zh_copy = go(copy(queries.at[me], queries.at[me], zh_send, zh_recv, zh=1 - zh))
    along_x_again(0)
    along_y_again(0)
    picks_arrived(1)
    picks_along(2)
    z_arrived(2)
    along_y(2)
    along_y_again(1)
    picks_arrived(2)
    picks_along(3)
    far_arrived(0)
    zh_copy.wait_recv()
    along_x(1)
    z_arrived(3)
    along_y(3)
    picks_arrived(3)
    picks_along(4)
    along_x_again(1)
    along_y_again(2)
    far_arrived(1)
    for k in range(ZH):
        for side in range(2):
            xhalf_copies[k, side].wait_recv()

    for m in range(SUBS):
        whole = queries[:, m].reshape(DRAWS, D)
        high, low = split(whole)
        parts_hi[m] = high
        parts_lo[m] = low
        query_half[m] = jnp.broadcast_to(0.5 * row_sums(whole * whole), (8, DRAWS))

    picks_arrived(4)
    along_y_again(3)
    far_arrived(2)

    band, spread = [], []
    for t in range(ROUNDS):
        index = jnp.full((1, DRAWS), bands[t], jnp.int32).astype(jnp.float32)
        band.append((D / 32.0) * (1.0 + index / 256.0))
        centre = jnp.concatenate([pick_out[5, 2 * t : 2 * t + 1], pick_out[5, 2 * t + 1 : 2 * t + 2]], 1)
        away = queries[:, x].reshape(DRAWS, D) - centre / MEMBERS
        spread.append(row_sums(away * away) / (2.0 * band[t]))

    far_arrived(3)
    for made in sib_copies:
        made.wait_recv()

    l_copies = []
    for n, m in enumerate((x_far, x_up, x_down, x)):
        high, low = parts_hi[m], parts_lo[m]
        shift = query_half[m, 0:1]
        for first in range(0, PAIRS, SLOTS):
            rows = []
            for s in range(first, first + SLOTS):
                p = table[m, s]
                rows.append(keys[lax.div(p, SUBS), lax.rem(p, SUBS)])
            rows = jnp.concatenate(rows, 0)
            norm_half = 0.5 * jnp.sum(rows * rows, -1, keepdims=True)
            key_high, key_low = split(rows)
            product = nt_dot(key_high, high) + nt_dot(key_low, high) + nt_dot(key_high, low)
            value = (product - norm_half).reshape(SLOTS, ROWS, DRAWS)
            peak = jnp.max(value, 1, keepdims=True)
            value = value - peak
            peak = peak.reshape(SLOTS, DRAWS) - shift
            for t in range(ROUNDS):
                rate = LOG2E / band[t]
                mass = jnp.sum(jnp.exp2(value * rate[None]), 1)
                sums_out[m, t, pl.ds(first, SLOTS)] = peak * rate + jnp.log2(mass)
        if n < X - 1:
            l_copies.append(go(copy(sums_out.at[m], sums_in.at[n], l_send.at[n], l_recv.at[n], x=m)))
        else:
            sums_in[n] = sums_out[m]

    for made in l_copies:
        made.wait_recv()
    pair_out[...] = log_sum(sums_in[...])
    pair_copy = go(copy(pair_out, pair_in, pair_send, pair_recv, zh=1 - zh))
    pair_copy.wait_recv()
    first, second = pair_out[...], pair_in[...]
    peak = jnp.maximum(first, second)
    whole = peak + jnp.log2(jnp.exp2(first - peak) + jnp.exp2(second - peak))
    for t in range(ROUNDS):
        logits = (LN2 / PAIRS) * jnp.sum(whole[t], 0, keepdims=True) - spread[t]
        logits = logits - jnp.max(logits, -1, keepdims=True)
        result = logits - jnp.log(jnp.sum(jnp.exp(logits), -1, keepdims=True))
        result = jnp.where(zh == 0, result[:, : X * ROWS], result[:, X * ROWS :])
        for k in range(X):
            final_out[k, t : t + 1, 0:ROWS] = result[:, k * ROWS : (k + 1) * ROWS]
    f_copies = []
    for n, k in enumerate((x_far, x_up, x_down)):
        f_copies.append(go(copy(final_out.at[k], final_in.at[x], f_send.at[n], f_recv.at[n], x=k)))
    final_in[x] = final_out[x]
    for made in f_copies:
        made.wait_recv()
    for m in range(SUBS):
        out[:, m] = final_in[m, 0:ROUNDS, 0:ROWS]
    for made in sends:
        made.wait_send()
    for k in range(ZL):
        z_sent(k)


def per_device(samples, pair_table, assignment, band_index):
    dma = pltpu.SemaphoreType.DMA
    smem = pl.BlockSpec(memory_space=pltpu.SMEM)
    vmem = pl.BlockSpec(memory_space=pltpu.VMEM)
    f32 = jnp.float32
    siblings = (Y + 1) * ZL
    return pl.pallas_call(
        kernel,
        name="weights",
        out_shape=jax.ShapeDtypeStruct((ROUNDS, SUBS, ROWS), f32),
        in_specs=[smem, smem, smem, vmem],
        out_specs=vmem,
        scratch_shapes=[
            pltpu.VMEM((Y * ZL * CORES, SUBS, ROWS, D), f32),
            pltpu.VMEM((GROUP, SUBS, ROWS, D), f32),
            pltpu.VMEM((SUBS, DRAWS, D), jnp.bfloat16),
            pltpu.VMEM((SUBS, DRAWS, D), jnp.bfloat16),
            pltpu.VMEM((SUBS, 8, DRAWS), f32),
            pltpu.VMEM((SUBS, ROUNDS, PAIRS, DRAWS), f32),
            pltpu.VMEM((X, ROUNDS, PAIRS, DRAWS), f32),
            pltpu.VMEM((ROUNDS, PAIRS, DRAWS), f32),
            pltpu.VMEM((ROUNDS, PAIRS, DRAWS), f32),
            pltpu.VMEM((6, 8, 128), f32),
            pltpu.VMEM((5, 3, 8, 128), f32),
            pltpu.VMEM((X, 8, 128), f32),
            pltpu.VMEM((X, 8, 128), f32),
            dma((ZL, 2)), dma((ZL,)),
            dma((ZL, 2)), dma((ZL, 2)),
            dma((ZL, 2)), dma((ZL, 2)),
            dma((siblings,)), dma((siblings,)),
            dma, dma,
            dma((ZH, 2)), dma((ZH, 2)),
            dma((ZH, 2)), dma((ZH, 2)),
            dma((5, 3)), dma((5, 3)),
            dma((X - 1,)), dma((X - 1,)),
            dma, dma,
            dma((X - 1,)), dma((X - 1,)),
        ],
        compiler_params=pltpu.CompilerParams(
            collective_id=0, has_side_effects=True, vmem_limit_bytes=48 * 1024 * 1024
        ),
    )(pair_table, assignment, band_index, samples)


def solution(mesh):
    finer = Mesh(mesh.devices.reshape(Y, ZL, CORES, ZH, X), NAMES)
    blk, grp = NAMES[:3], NAMES[3:]
    return jax.shard_map(
        per_device,
        mesh=finer,
        in_specs=(P(blk, grp, None), P(blk, None), P(None, blk), P()),
        out_specs=P(None, blk, grp),
        check_vma=False,
    )
```

time: 61.5 us -> 56.8 us (0.924)
  Pallas kernels: 57.8 us -> 53.1 us
    pallas_call x1, Pallas kernels: 57.8 us -> 53.1 us  [per_device(): pl.pallas_call(kernel, name='weights', out_shape=jax.ShapeDtypeStruct((RO...]
where the time goes in v2:
time: 56.8 us; the launch traced here: 56.6 us
  Pallas kernels  53.1 us (93%)
  local copies, waits for them, and re-layouts  3.51 us (6%)
    pallas_call x1, Pallas kernels, per_device(): pl.pallas_call(kernel, name='weights', out_shape=jax.ShapeDtypeStruct((RO...  53.1 us
    unnamed x9, local copies, waits for them, and re-layouts  3.51 us

profile of v2, /device:TPU:1, one launch (start us, length us, event | category | flops | bytes accessed | tf_op | source)
XLA Modules:
  0.0 56.6 jit_solution(10675011736682511647)
XLA Ops:
  0.0 0.0 copy-start
  0.0 0.9 %copy-done = f32[4,32,256]{2,1,0:T(8,128)S(1)} copy-done((f32[4,32,256]{2,1,0:T(8,128)S(1)}, f32[4,32,256]{2,1,0:T(8,128)}, u32[]{:S(2)}) %copy-start) | copy-done | bytes 131096
  0.9 0.0 copy-start.1
  0.9 0.7 %copy-done.1 = s32[4,16]{1,0:T(4,128)S(1)} copy-done((s32[4,16]{1,0:T(4,128)S(1)}, s32[4,16]{1,0:T(4,128)}, u32[]{:S(2)}) %copy-start.1) | copy-done | bytes 280
  1.6 0.0 copy-start.2
  1.6 0.7 %copy-done.2 = s32[2,4]{1,0:T(2,128)S(1)} copy-done((s32[2,4]{1,0:T(2,128)S(1)}, s32[2,4]{1,0:T(2,128)}, u32[]{:S(2)}) %copy-start.2) | copy-done | bytes 56
  2.3 0.0 copy-start.3
  2.3 0.7 %copy-done.3 = s32[2]{0:T(128)S(1)} copy-done((s32[2]{0:T(128)S(1)}, s32[2]{0:T(128)}, u32[]{:S(2)}) %copy-start.3) | copy-done | bytes 32
  2.9 53.1 %weights.1 = f32[2,4,32]{2,1,0:T(4,128)S(1)} custom-call(s32[4,16]{1,0:T(4,128)S(1)} %copy-done.1, s32[2,4]{1,0:T(2,128)S(1)} %copy-done.2, s32[2]{0:T(128)S(1)} %copy-done.3, f32[4,32,256]{2,1,0:T(8,128)S(1)} %copy-done), custom_call_target="tpu_custom_call" | custom-call | tf_op jit(solution)/shard_map/weights/pallas_call | solution.py:317
  56.0 0.6 %copy.6 = f32[2,4,32]{2,1,0:T(4,128)} copy(f32[2,4,32]{2,1,0:T(4,128)S(1)} %weights.1) | data formatting | bytes 2048
Async XLA Ops:
  0.0 0.9 %copy-start = (f32[4,32,256]{2,1,0:T(8,128)S(1)}, f32[4,32,256]{2,1,0:T(8,128)}, u32[]{:S(2)}) copy-start(f32[4,32,256]{2,1,0:T(8,128)} %own.1) | copy-start | bytes 393220
  0.9 0.7 %copy-start.1 = (s32[4,16]{1,0:T(4,128)S(1)}, s32[4,16]{1,0:T(4,128)}, u32[]{:S(2)}) copy-start(s32[4,16]{1,0:T(4,128)} %table.1) | copy-start | bytes 772
  1.6 0.7 %copy-start.2 = (s32[2,4]{1,0:T(2,128)S(1)}, s32[2,4]{1,0:T(2,128)}, u32[]{:S(2)}) copy-start(s32[2,4]{1,0:T(2,128)} %picks.1) | copy-start | bytes 100
  2.3 0.7 %copy-start.3 = (s32[2]{0:T(128)S(1)}, s32[2]{0:T(128)}, u32[]{:S(2)}) copy-start(s32[2]{0:T(128)} %bands.1) | copy-start | bytes 28

commit v3 on v2

v3 whole, which is shorter than its diff:
```python
import math

import jax
import jax.numpy as jnp
from jax import lax
from jax.experimental import pallas as pl
from jax.experimental.pallas import tpu as pltpu
from jax.sharding import Mesh
from jax.sharding import PartitionSpec as P

MESH = pl.DeviceIdType.MESH
NAMES = ("y", "zl", "core", "zh", "x")
Y, ZL, CORES, ZH, X = 4, 4, 2, 2, 4
GROUP = ZH * X
SUBS, ROWS, D, ROUNDS, PAIRS, MEMBERS = 4, 32, 256, 2, 16, 128
DRAWS = GROUP * ROWS
HALF = SUBS // 2
SLOTS = 8
PIECES = 2
LOG2E = math.log2(math.e)
LN2 = math.log(2.0)
NT = (((1,), (1,)), ((), ()))


def split(value):
    high = value.astype(jnp.bfloat16)
    low = (value - high.astype(jnp.float32)).astype(jnp.bfloat16)
    return high, low


def nt_dot(a, b):
    return lax.dot_general(a, b, NT, preferred_element_type=jnp.float32)


def row_sums(value):
    ones = jnp.ones((8, value.shape[1]), jnp.bfloat16)
    high, low = split(value)
    lowest = (value - high.astype(jnp.float32) - low.astype(jnp.float32)).astype(jnp.bfloat16)
    return (nt_dot(ones, high) + nt_dot(ones, low) + nt_dot(ones, lowest))[0:1]


def log_sum(pieces):
    peak = jnp.max(pieces, 0)
    return peak + jnp.log2(jnp.sum(jnp.exp2(pieces - peak[None]), 0))


def kernel(
    table_hbm, picks_hbm, bands_hbm, own, out,
    table, picks, bands,
    keys, queries, parts_hi, parts_lo, query_half, sums_out, sums_in, pair_out, pair_in,
    pick_out, pick_in, final_out, final_in, local_sem,
    z_send, z_recv, y_send, y_recv, half_send, half_recv, sib_send, sib_recv,
    r_send, r_recv, x_send, x_recv, xhalf_send, xhalf_recv,
    p_send, p_recv, l_send, l_recv, pair_send, pair_recv, f_send, f_recv,
):
    y, zl, core, zh, x = (lax.axis_index(name) for name in NAMES)
    me = zh * X + x

    def block(row, seg):
        return (row * ZL + seg) * CORES + core

    def copy(src, dst, send, recv, **where):
        return pltpu.make_async_remote_copy(
            src_ref=src, dst_ref=dst, send_sem=send, recv_sem=recv, device_id=where, device_id_type=MESH
        )

    y_up, y_down, y_far = (lax.rem(y + k, Y) for k in (1, 3, 2))
    x_up, x_down, x_far = (lax.rem(x + k, X) for k in (1, 3, 2))

    bottom, top = zl == 0, zl == ZL - 1
    z_up = {"zl": lax.rem(zl + 1, ZL), "zh": jnp.where(top, 1 - zh, zh)}
    z_down = {"zl": lax.rem(zl + ZL - 1, ZL), "zh": jnp.where(bottom, 1 - zh, zh)}
    barrier = pltpu.get_barrier_semaphore()
    greeted = [{"core": 1 - core}, z_up, z_down]
    greeted += [{"y": k} for k in (y_up, y_down)]
    greeted += [{"x": k} for k in (x_up, x_down)]
    for where in greeted:
        pl.semaphore_signal(barrier, inc=1, device_id=where, device_id_type=MESH)

    mine = block(y, zl)
    local = [
        pltpu.make_async_copy(src, dst, local_sem.at[n])
        for n, (src, dst) in enumerate(
            ((picks_hbm, picks), (own, keys.at[mine]), (own, queries.at[me]), (table_hbm, table), (bands_hbm, bands))
        )
    ]
    for made in local:
        made.start()

    sends = []

    def go(made):
        made.start()
        sends.append(made)
        return made

    low = zl < 2
    segs = [zl, zl + 1 - 2 * lax.rem(zl, 2), jnp.where(low, 2, 1), jnp.where(low, 3, 0)]
    y_copies, half_copies, sib_copies = {}, {}, []

    def piece(b, c, side=None):
        each = SUBS // PIECES
        if side is None:
            return b, pl.ds(c * each, each)
        if each > 1:
            return b, pl.ds(c * each + side * (each // 2), each // 2)
        return b, c, pl.ds(side * (ROWS // 2), ROWS // 2)

    def to_sibling(*where):
        n = len(sib_copies)
        part = keys.at[where]
        sib_copies.append(go(copy(part, part, sib_send.at[n], sib_recv.at[n], core=1 - core)))

    def z_copy(seg, c, up, fresh=False):
        where = piece(block(y, seg), c)
        return copy(
            own.at[where[1:]] if fresh else keys.at[where], keys.at[where],
            z_send.at[seg, c, int(up)], z_recv.at[seg, c], zl=zl + 1 if up else zl - 1,
        )

    def relay(seg, far, up, fresh=False, crossing=False):
        c = 0 if up else 1
        there = piece(block(Y, seg), c)
        here = piece(block(y, seg), c) if crossing else there
        return copy(
            own.at[here[1:]] if fresh else keys.at[here], keys.at[there],
            r_send.at[far, c], r_recv.at[far, c], **(z_up if up else z_down),
        )

    def along_y(k, c):
        where = piece(block(y, segs[k]), c)
        for side, to in enumerate((y_up, y_down)):
            y_copies[k, c, side] = go(
                copy(
                    own.at[where[1:]] if k == 0 else keys.at[where], keys.at[where], y_send.at[k, c, side], y_recv.at[k, c, side], y=to
                )
            )
        if k:
            to_sibling(*where)

    def along_y_again(k, c):
        for side, (origin, to) in enumerate(((y_down, y_up), (y_up, y_down))):
            b = block(origin, segs[k])
            y_copies[k, c, side].wait_recv()
            part = keys.at[piece(b, c, side)]
            half_copies[k, c, side] = go(
                copy(part, part, half_send.at[k, c, side], half_recv.at[k, c, side], y=to)
            )
            to_sibling(*piece(b, c))

    def far_arrived(k, c):
        for side in range(2):
            half_copies[k, c, side].wait_recv()
        to_sibling(*piece(block(y_far, segs[k]), c))

    def z_onward(k, c, act):
        seg, fresh = segs[k], k == 0

        @pl.when((seg <= zl) & ~top)
        def _():
            act(z_copy(seg, c, True, fresh))

        @pl.when((seg >= zl) & ~bottom)
        def _():
            act(z_copy(seg, c, False, fresh))

        if c == 0:

            @pl.when((seg <= zl) & top)
            def _():
                act(relay(seg, zl - seg, True, fresh, True))

        if c == PIECES - 1:

            @pl.when((seg >= zl) & bottom)
            def _():
                act(relay(seg, seg - zl, False, fresh, True))

    def z_arrived(k, c):
        z_copy(segs[k], c, True).wait_recv()
        z_onward(k, c, lambda made: made.start())

    def relay_onward(n, act, arrived):
        for up in (True, False):
            seg = lax.rem(zl + ZL - n, ZL) if up else lax.rem(zl + n, ZL)

            @pl.when(zl < n if up else ZL - 1 - zl < n)
            def _():
                if arrived:
                    relay(seg, n - 1, up).wait_recv()
                if n < ZL:
                    act(relay(seg, n, up))

    def relayed(n):
        relay_onward(n, lambda made: made.start(), True)

    x_copies, xhalf_copies = {}, {}

    def along_x(k):
        slot = lax.rem(zh + k, ZH) * X + x
        for side, to in enumerate((x_up, x_down)):
            x_copies[k, side] = go(
                copy(
                    queries.at[slot] if k else own, queries.at[slot],
                    x_send.at[k, side], x_recv.at[k, side], x=to,
                )
            )

    def along_x_again(k):
        for side, (origin, to) in enumerate(((x_down, x_up), (x_up, x_down))):
            slot = lax.rem(zh + k, ZH) * X + origin
            x_copies[k, side].wait_recv()
            part = queries.at[slot, pl.ds(side * HALF, HALF)]
            xhalf_copies[k, side] = go(copy(part, part, xhalf_send.at[k, side], xhalf_recv.at[k, side], x=to))

    def prepare(k):
        for side in range(2):
            xhalf_copies[k, side].wait_recv()
        half = lax.rem(zh + k, ZH)
        these = pl.ds(pl.multiple_of(half * X * ROWS, X * ROWS), X * ROWS)
        for m in range(SUBS):
            rows = queries[pl.ds(half * X, X), m].reshape(X * ROWS, D)
            high, low = split(rows)
            parts_hi[m, these] = high
            parts_lo[m, these] = low
            query_half[m, :, these] = jnp.broadcast_to(0.5 * row_sums(rows * rows), (8, X * ROWS))

    axes = [
        [{"core": 1 - core}],
        [{"zl": lax.rem(zl + k, ZL)} for k in range(1, ZL)],
        [{"y": lax.rem(y + k, Y)} for k in range(1, Y)],
        [{"x": lax.rem(x + k, X)} for k in range(1, X)],
        [{"zh": 1 - zh}],
    ]
    pick_copies = {}

    def picks_along(a):
        for n, where in enumerate(axes[a]):
            pick_copies[a, n] = go(
                copy(pick_out.at[a], pick_in.at[a, n], p_send.at[a, n], p_recv.at[a, n], **where)
            )

    def picks_arrived(a):
        total = pick_out[a]
        for n in range(len(axes[a])):
            pick_copies[a, n].wait_recv()
            total += pick_in[a, n]
        pick_out[a + 1] = total

    every = range(PIECES)
    pl.semaphore_wait(barrier, len(greeted))
    for c in every:
        z_onward(0, c, lambda made: made.start())
        along_y(0, c)
    along_x(0)

    for made in local[:3]:
        made.wait()
    to_sibling(mine)
    number = lax.broadcasted_iota(jnp.int32, (ROWS, D), 0)
    pick_out[0] = jnp.zeros((8, 128), jnp.float32)
    for t in range(ROUNDS):
        total = jnp.zeros((ROWS, D), jnp.float32)
        for m in range(SUBS):
            total += jnp.where(number == picks[t, m] - me * ROWS, queries[me, m], 0.0)
        total = jnp.sum(total, 0, keepdims=True)
        for side in range(2):
            pick_out[0, 2 * t + side : 2 * t + side + 1] = total[:, 128 * side : 128 * side + 128]
    picks_along(0)

    for c in every:
        z_arrived(1, c)
        along_y(1, c)
    relayed(1)
    for c in every:
        along_y_again(0, c)
    along_x_again(0)
    for c in every:
        z_arrived(2, c)
        along_y(2, c)
    relayed(2)
    for c in every:
        along_y_again(1, c)
    for c in every:
        z_arrived(3, c)
        along_y(3, c)
    relayed(3)
    for c in every:
        far_arrived(0, c)
    for c in every:
        along_y_again(2, c)
    picks_arrived(0)
    picks_along(1)
    prepare(0)
    relayed(4)
    queries[(1 - zh) * X + x] = keys[block(Y, zl)]
    along_x(1)
    picks_arrived(1)
    picks_along(2)
    for c in every:
        far_arrived(1, c)
    picks_arrived(2)
    picks_along(3)
    for c in every:
        along_y_again(3, c)
    along_x_again(1)
    for c in every:
        far_arrived(2, c)
    picks_arrived(3)
    picks_along(4)
    prepare(1)

    for made in local[3:]:
        made.wait()

    band = []
    for t in range(ROUNDS):
        index = jnp.full((1, DRAWS), bands[t], jnp.int32).astype(jnp.float32)
        band.append((D / 32.0) * (1.0 + index / 256.0))
    for c in every:
        far_arrived(3, c)
    for made in sib_copies:
        made.wait_recv()

    l_copies = []
    for n, m in enumerate((x_far, x_up, x_down, x)):
        high, low = parts_hi[m], parts_lo[m]
        shift = query_half[m, 0:1]
        for first in range(0, PAIRS, SLOTS):
            rows = []
            for s in range(first, first + SLOTS):
                p = table[m, s]
                rows.append(keys[lax.div(p, SUBS), lax.rem(p, SUBS)])
            rows = jnp.concatenate(rows, 0)
            norm_half = 0.5 * jnp.sum(rows * rows, -1, keepdims=True)
            key_high, key_low = split(rows)
            product = nt_dot(key_high, high) + nt_dot(key_low, high) + nt_dot(key_high, low)
            value = (product - norm_half).reshape(SLOTS, ROWS, DRAWS)
            peak = jnp.max(value, 1, keepdims=True)
            value = value - peak
            peak = peak.reshape(SLOTS, DRAWS) - shift
            for t in range(ROUNDS):
                rate = LOG2E / band[t]
                mass = jnp.sum(jnp.exp2(value * rate[None]), 1)
                sums_out[m, t, pl.ds(first, SLOTS)] = peak * rate + jnp.log2(mass)
        if n < X - 1:
            l_copies.append(go(copy(sums_out.at[m], sums_in.at[n], l_send.at[n], l_recv.at[n], x=m)))
        else:
            sums_in[n] = sums_out[m]

    for made in l_copies:
        made.wait_recv()
    pair_out[...] = log_sum(sums_in[...])
    pair_copy = go(copy(pair_out, pair_in, pair_send, pair_recv, zh=1 - zh))
    spread = []
    picks_arrived(4)
    for t in range(ROUNDS):
        centre = jnp.concatenate([pick_out[5, 2 * t : 2 * t + 1], pick_out[5, 2 * t + 1 : 2 * t + 2]], 1)
        away = queries[:, x].reshape(DRAWS, D) - centre / MEMBERS
        spread.append(row_sums(away * away) / (2.0 * band[t]))
    pair_copy.wait_recv()
    first, second = pair_out[...], pair_in[...]
    peak = jnp.maximum(first, second)
    whole = peak + jnp.log2(jnp.exp2(first - peak) + jnp.exp2(second - peak))
    for t in range(ROUNDS):
        logits = (LN2 / PAIRS) * jnp.sum(whole[t], 0, keepdims=True) - spread[t]
        logits = logits - jnp.max(logits, -1, keepdims=True)
        result = logits - jnp.log(jnp.sum(jnp.exp(logits), -1, keepdims=True))
        result = jnp.where(zh == 0, result[:, : X * ROWS], result[:, X * ROWS :])
        for k in range(X):
            final_out[k, t : t + 1, 0:ROWS] = result[:, k * ROWS : (k + 1) * ROWS]
    f_copies = []
    for n, k in enumerate((x_far, x_up, x_down)):
        f_copies.append(go(copy(final_out.at[k], final_in.at[x], f_send.at[n], f_recv.at[n], x=k)))
    final_in[x] = final_out[x]
    for made in f_copies:
        made.wait_recv()
    for m in range(SUBS):
        out[:, m] = final_in[m, 0:ROUNDS, 0:ROWS]
    for made in sends:
        made.wait_send()
    for k in range(ZL):
        for c in every:
            z_onward(k, c, lambda made: made.wait_send())
        if k:
            relay_onward(k, lambda made: made.wait_send(), False)


def per_device(samples, pair_table, assignment, band_index):
    dma = pltpu.SemaphoreType.DMA
    hbm = pl.BlockSpec(memory_space=pltpu.HBM)
    vmem = pl.BlockSpec(memory_space=pltpu.VMEM)
    f32 = jnp.float32
    siblings = 1 + (Y * ZL - 1) * PIECES
    return pl.pallas_call(
        kernel,
        name="weights",
        out_shape=jax.ShapeDtypeStruct((ROUNDS, SUBS, ROWS), f32),
        in_specs=[hbm] * 4,
        out_specs=vmem,
        scratch_shapes=[
            pltpu.SMEM((SUBS, PAIRS), jnp.int32),
            pltpu.SMEM((ROUNDS, SUBS), jnp.int32),
            pltpu.SMEM((ROUNDS,), jnp.int32),
            pltpu.VMEM(((Y + 1) * ZL * CORES, SUBS, ROWS, D), f32),
            pltpu.VMEM((GROUP, SUBS, ROWS, D), f32),
            pltpu.VMEM((SUBS, DRAWS, D), jnp.bfloat16),
            pltpu.VMEM((SUBS, DRAWS, D), jnp.bfloat16),
            pltpu.VMEM((SUBS, 8, DRAWS), f32),
            pltpu.VMEM((SUBS, ROUNDS, PAIRS, DRAWS), f32),
            pltpu.VMEM((X, ROUNDS, PAIRS, DRAWS), f32),
            pltpu.VMEM((ROUNDS, PAIRS, DRAWS), f32),
            pltpu.VMEM((ROUNDS, PAIRS, DRAWS), f32),
            pltpu.VMEM((6, 8, 128), f32),
            pltpu.VMEM((5, 3, 8, 128), f32),
            pltpu.VMEM((X, 8, 128), f32),
            pltpu.VMEM((X, 8, 128), f32),
            dma((5,)),
            dma((ZL, PIECES, 2)), dma((ZL, PIECES)),
            dma((ZL, PIECES, 2)), dma((ZL, PIECES, 2)),
            dma((ZL, PIECES, 2)), dma((ZL, PIECES, 2)),
            dma((siblings,)), dma((siblings,)),
            dma((ZL, 2)), dma((ZL, 2)),
            dma((ZH, 2)), dma((ZH, 2)),
            dma((ZH, 2)), dma((ZH, 2)),
            dma((5, 3)), dma((5, 3)),
            dma((X - 1,)), dma((X - 1,)),
            dma, dma,
            dma((X - 1,)), dma((X - 1,)),
        ],
        compiler_params=pltpu.CompilerParams(
            collective_id=0, has_side_effects=True, vmem_limit_bytes=60 * 1024 * 1024
        ),
    )(pair_table, assignment, band_index, samples)


def solution(mesh):
    finer = Mesh(mesh.devices.reshape(Y, ZL, CORES, ZH, X), NAMES)
    blk, grp = NAMES[:3], NAMES[3:]
    return jax.shard_map(
        per_device,
        mesh=finer,
        in_specs=(P(blk, grp, None), P(blk, None), P(None, blk), P()),
        out_specs=P(None, blk, grp),
        check_vma=False,
    )
```

time: 56.8 us -> 52.5 us (0.924)
  local copies, waits for them, and re-layouts: 3.51 us -> 1.28 us
  Pallas kernels: 53.1 us -> 51.1 us
    unnamed x9 -> x1, local copies, waits for them, and re-layouts: 3.51 us -> 1.28 us
    pallas_call x1, Pallas kernels: 53.1 us -> 51.1 us  [per_device(): pl.pallas_call(kernel, name='weights', out_shape=jax.ShapeDtypeStruct((RO...]
where the time goes in v3:
time: 52.5 us; the launch traced here: 52.4 us
  Pallas kernels  51.1 us (97%)
  local copies, waits for them, and re-layouts  1.28 us (2%)
    pallas_call x1, Pallas kernels, per_device(): pl.pallas_call(kernel, name='weights', out_shape=jax.ShapeDtypeStruct((RO...  51.1 us
    unnamed x1, local copies, waits for them, and re-layouts  1.28 us

profile of v3, /device:TPU:1, one launch (start us, length us, event | category | flops | bytes accessed | tf_op | source)
XLA Modules:
  0.0 52.4 jit_solution(7495134657557839503)
XLA Ops:
  0.0 51.1 %weights.1 = f32[2,4,32]{2,1,0:T(4,128)} custom-call(s32[4,16]{1,0:T(4,128)} %table_hbm.1, s32[2,4]{1,0:T(2,128)} %picks_hbm.1, s32[2]{0:T(128)} %bands_hbm.1, f32[4,32,256]{2,1,0:T(8,128)} %own.1), custom_call_target="tpu_custom_call" | custom-call | tf_op jit(solution)/shard_map/weights/pallas_call | solution.py:395
  51.1 1.3 %copy.6 = f32[2,4,32]{2,1,0:T(4,128)} copy(f32[2,4,32]{2,1,0:T(4,128)} %weights.1) | data formatting | bytes 2048

commit v4 on v3

--- a/solution.py
+++ b/solution.py
@@ -47,10 +47,10 @@
 def kernel(
     table_hbm, picks_hbm, bands_hbm, own, out,
     table, picks, bands,
-    keys, queries, parts_hi, parts_lo, query_half, sums_out, sums_in, pair_out, pair_in,
+    keys, queries, parts, query_half, sums_out, sums_in, pair_out, pair_in,
     pick_out, pick_in, final_out, final_in, local_sem,
     z_send, z_recv, y_send, y_recv, half_send, half_recv, sib_send, sib_recv,
-    r_send, r_recv, x_send, x_recv, xhalf_send, xhalf_recv,
+    r_send, r_recv, x_send, x_recv,
     p_send, p_recv, l_send, l_recv, pair_send, pair_recv, f_send, f_recv,
 ):
     y, zl, core, zh, x = (lax.axis_index(name) for name in NAMES)
@@ -73,7 +73,7 @@
     barrier = pltpu.get_barrier_semaphore()
     greeted = [{"core": 1 - core}, z_up, z_down]
     greeted += [{"y": k} for k in (y_up, y_down)]
-    greeted += [{"x": k} for k in (x_up, x_down)]
+    greeted += [{"x": k} for k in (x_up, x_down, x_far)]
     for where in greeted:
         pl.semaphore_signal(barrier, inc=1, device_id=where, device_id_type=MESH)
 
@@ -194,35 +194,28 @@
     def relayed(n):
         relay_onward(n, lambda made: made.start(), True)
 
-    x_copies, xhalf_copies = {}, {}
-
-    def along_x(k):
-        slot = lax.rem(zh + k, ZH) * X + x
-        for side, to in enumerate((x_up, x_down)):
-            x_copies[k, side] = go(
+    x_copies = {}
+
+    def along_x(k, c):
+        where = piece(lax.rem(zh + k, ZH) * X + x, c)
+        for n, to in enumerate((x_far, x_up, x_down)):
+            x_copies[k, c, n] = go(
                 copy(
-                    queries.at[slot] if k else own, queries.at[slot],
-                    x_send.at[k, side], x_recv.at[k, side], x=to,
+                    queries.at[where] if k else own.at[where[1:]], queries.at[where],
+                    x_send.at[k, c, n], x_recv.at[k, c, n], x=to,
                 )
             )
 
-    def along_x_again(k):
-        for side, (origin, to) in enumerate(((x_down, x_up), (x_up, x_down))):
-            slot = lax.rem(zh + k, ZH) * X + origin
-            x_copies[k, side].wait_recv()
-            part = queries.at[slot, pl.ds(side * HALF, HALF)]
-            xhalf_copies[k, side] = go(copy(part, part, xhalf_send.at[k, side], xhalf_recv.at[k, side], x=to))
-
     def prepare(k):
-        for side in range(2):
-            xhalf_copies[k, side].wait_recv()
+        for c in range(PIECES):
+            for n in range(X - 1):
+                x_copies[k, c, n].wait_recv()
         half = lax.rem(zh + k, ZH)
         these = pl.ds(pl.multiple_of(half * X * ROWS, X * ROWS), X * ROWS)
         for m in range(SUBS):
             rows = queries[pl.ds(half * X, X), m].reshape(X * ROWS, D)
             high, low = split(rows)
-            parts_hi[m, these] = high
-            parts_lo[m, these] = low
+            parts[m, these] = jnp.concatenate([high, high, low], 1)
             query_half[m, :, these] = jnp.broadcast_to(0.5 * row_sums(rows * rows), (8, X * ROWS))
 
     axes = [
@@ -252,7 +245,8 @@
     for c in every:
         z_onward(0, c, lambda made: made.start())
         along_y(0, c)
-    along_x(0)
+    for c in every:
+        along_x(0, c)
 
     for made in local[:3]:
         made.wait()
@@ -274,7 +268,6 @@
     relayed(1)
     for c in every:
         along_y_again(0, c)
-    along_x_again(0)
     for c in every:
         z_arrived(2, c)
         along_y(2, c)
@@ -285,29 +278,27 @@
         z_arrived(3, c)
         along_y(3, c)
     relayed(3)
-    for c in every:
-        far_arrived(0, c)
-    for c in every:
-        along_y_again(2, c)
     picks_arrived(0)
     picks_along(1)
+    for c in every:
+        far_arrived(0, c)
+    for c in every:
+        along_y_again(2, c)
+    picks_arrived(1)
+    picks_along(2)
     prepare(0)
     relayed(4)
     queries[(1 - zh) * X + x] = keys[block(Y, zl)]
-    along_x(1)
-    picks_arrived(1)
-    picks_along(2)
+    for c in every:
+        along_x(1, c)
     for c in every:
         far_arrived(1, c)
     picks_arrived(2)
     picks_along(3)
     for c in every:
         along_y_again(3, c)
-    along_x_again(1)
     for c in every:
         far_arrived(2, c)
-    picks_arrived(3)
-    picks_along(4)
     prepare(1)
 
     for made in local[3:]:
@@ -322,9 +313,10 @@
     for made in sib_copies:
         made.wait_recv()
 
+    picks_arrived(3)
+    picks_along(4)
     l_copies = []
     for n, m in enumerate((x_far, x_up, x_down, x)):
-        high, low = parts_hi[m], parts_lo[m]
         shift = query_half[m, 0:1]
         for first in range(0, PAIRS, SLOTS):
             rows = []
@@ -334,7 +326,7 @@
             rows = jnp.concatenate(rows, 0)
             norm_half = 0.5 * jnp.sum(rows * rows, -1, keepdims=True)
             key_high, key_low = split(rows)
-            product = nt_dot(key_high, high) + nt_dot(key_low, high) + nt_dot(key_high, low)
+            product = nt_dot(jnp.concatenate([key_high, key_low, key_high], 1), parts[m])
             value = (product - norm_half).reshape(SLOTS, ROWS, DRAWS)
             peak = jnp.max(value, 1, keepdims=True)
             value = value - peak
@@ -358,6 +350,13 @@
         centre = jnp.concatenate([pick_out[5, 2 * t : 2 * t + 1], pick_out[5, 2 * t + 1 : 2 * t + 2]], 1)
         away = queries[:, x].reshape(DRAWS, D) - centre / MEMBERS
         spread.append(row_sums(away * away) / (2.0 * band[t]))
+    while sends[0] is not pair_copy:
+        sends.pop(0).wait_send()
+    for k in range(ZL):
+        for c in every:
+            z_onward(k, c, lambda made: made.wait_send())
+        if k:
+            relay_onward(k, lambda made: made.wait_send(), False)
     pair_copy.wait_recv()
     first, second = pair_out[...], pair_in[...]
     peak = jnp.maximum(first, second)
@@ -379,11 +378,6 @@
         out[:, m] = final_in[m, 0:ROUNDS, 0:ROWS]
     for made in sends:
         made.wait_send()
-    for k in range(ZL):
-        for c in every:
-            z_onward(k, c, lambda made: made.wait_send())
-        if k:
-            relay_onward(k, lambda made: made.wait_send(), False)
 
 
 def per_device(samples, pair_table, assignment, band_index):
@@ -404,8 +398,7 @@
             pltpu.SMEM((ROUNDS,), jnp.int32),
             pltpu.VMEM(((Y + 1) * ZL * CORES, SUBS, ROWS, D), f32),
             pltpu.VMEM((GROUP, SUBS, ROWS, D), f32),
-            pltpu.VMEM((SUBS, DRAWS, D), jnp.bfloat16),
-            pltpu.VMEM((SUBS, DRAWS, D), jnp.bfloat16),
+            pltpu.VMEM((SUBS, DRAWS, 3 * D), jnp.bfloat16),
             pltpu.VMEM((SUBS, 8, DRAWS), f32),
             pltpu.VMEM((SUBS, ROUNDS, PAIRS, DRAWS), f32),
             pltpu.VMEM((X, ROUNDS, PAIRS, DRAWS), f32),
@@ -421,8 +414,7 @@
             dma((ZL, PIECES, 2)), dma((ZL, PIECES, 2)),
             dma((siblings,)), dma((siblings,)),
             dma((ZL, 2)), dma((ZL, 2)),
-            dma((ZH, 2)), dma((ZH, 2)),
-            dma((ZH, 2)), dma((ZH, 2)),
+            dma((ZH, PIECES, X - 1)), dma((ZH, PIECES, X - 1)),
             dma((5, 3)), dma((5, 3)),
             dma((X - 1,)), dma((X - 1,)),
             dma, dma,

time: 52.5 us -> 51.2 us (0.975)
  Pallas kernels: 51.1 us -> 49.9 us
    pallas_call x1, Pallas kernels: 51.1 us -> 49.9 us  [per_device(): pl.pallas_call(kernel, name='weights', out_shape=jax.ShapeDtypeStruct((RO...]
where the time goes in v4:
time: 51.2 us; the launch traced here: 51.1 us
  Pallas kernels  49.9 us (97%)
  local copies, waits for them, and re-layouts  1.28 us (2%)
    pallas_call x1, Pallas kernels, per_device(): pl.pallas_call(kernel, name='weights', out_shape=jax.ShapeDtypeStruct((RO...  49.9 us
    unnamed x1, local copies, waits for them, and re-layouts  1.28 us

profile of v4, /device:TPU:1, one launch (start us, length us, event | category | flops | bytes accessed | tf_op | source)
XLA Modules:
  0.0 51.1 jit_solution(17521000248536077136)
XLA Ops:
  0.0 49.9 %weights.1 = f32[2,4,32]{2,1,0:T(4,128)} custom-call(s32[4,16]{1,0:T(4,128)} %table_hbm.1, s32[2,4]{1,0:T(2,128)} %picks_hbm.1, s32[2]{0:T(128)} %bands_hbm.1, f32[4,32,256]{2,1,0:T(8,128)} %own.1), custom_call_target="tpu_custom_call" | custom-call | tf_op jit(solution)/shard_map/weights/pallas_call | solution.py:389
  49.9 1.3 %copy.6 = f32[2,4,32]{2,1,0:T(4,128)} copy(f32[2,4,32]{2,1,0:T(4,128)} %weights.1) | data formatting | bytes 2048

commit v5 on v4

--- a/solution.py
+++ b/solution.py
@@ -267,10 +267,10 @@
         along_y(1, c)
     relayed(1)
     for c in every:
-        along_y_again(0, c)
-    for c in every:
         z_arrived(2, c)
         along_y(2, c)
+    for c in every:
+        along_y_again(0, c)
     relayed(2)
     for c in every:
         along_y_again(1, c)
@@ -280,23 +280,23 @@
     relayed(3)
     picks_arrived(0)
     picks_along(1)
+    relayed(4)
+    queries[(1 - zh) * X + x] = keys[block(Y, zl)]
+    for c in every:
+        along_x(1, c)
+    for c in every:
+        along_y_again(2, c)
     for c in every:
         far_arrived(0, c)
-    for c in every:
-        along_y_again(2, c)
     picks_arrived(1)
     picks_along(2)
     prepare(0)
-    relayed(4)
-    queries[(1 - zh) * X + x] = keys[block(Y, zl)]
-    for c in every:
-        along_x(1, c)
+    for c in every:
+        along_y_again(3, c)
     for c in every:
         far_arrived(1, c)
     picks_arrived(2)
     picks_along(3)
-    for c in every:
-        along_y_again(3, c)
     for c in every:
         far_arrived(2, c)
     prepare(1)

time: 51.2 us -> 50.4 us (0.984)
  the two profiles are of different devices: /device:TPU:1 before, /device:TPU:2 now
where the time goes in v5:
time: 50.4 us; the launch traced here: 50.2 us
  Pallas kernels  49 us (97%)
  local copies, waits for them, and re-layouts  1.28 us (3%)
    pallas_call x1, Pallas kernels, per_device(): pl.pallas_call(kernel, name='weights', out_shape=jax.ShapeDtypeStruct((RO...  49 us
    unnamed x1, local copies, waits for them, and re-layouts  1.28 us

profile of v5, /device:TPU:2, one launch (start us, length us, event | category | flops | bytes accessed | tf_op | source)
XLA Modules:
  0.0 50.2 jit_solution(7751048369163095442)
XLA Ops:
  0.0 49.0 %weights.1 = f32[2,4,32]{2,1,0:T(4,128)} custom-call(s32[4,16]{1,0:T(4,128)} %table_hbm.1, s32[2,4]{1,0:T(2,128)} %picks_hbm.1, s32[2]{0:T(128)} %bands_hbm.1, f32[4,32,256]{2,1,0:T(8,128)} %own.1), custom_call_target="tpu_custom_call" | custom-call | tf_op jit(solution)/shard_map/weights/pallas_call | solution.py:389
  49.0 1.3 %copy.6 = f32[2,4,32]{2,1,0:T(4,128)} copy(f32[2,4,32]{2,1,0:T(4,128)} %weights.1) | data formatting | bytes 2048
